TPU v7x, 32 devices: a whole 2x2x4 slice. The times are simulated.
32 devices in a mesh: elem: 16 (over z, x, core), mode: 2 (over y).
Axes of the slice: x: 2, y: 2, z: 4, core: 2. Of those that a mesh axis runs over, the one named last changes fastest.
Arguments:
- velocity: float32 [1024, 128, 128], P(None, ('elem', 'mode')), may hold values from -6 to 6
- previous: float32 [1024, 128, 128], P('mode', 'elem'), may hold values from -6 to 6
- derivative: float32 [128, 128], replicated, may hold values from -0.5 to 0.5
- stiffness: float32 [128, 128], replicated, as said below
- coupling: float32 [4, 128, 128], replicated, may hold values from -0.25 to 0.25
- reaction: float32 [128], P('elem'), may hold values from 0.5 to 4
- axial_weight: float32 [128], P('elem'), may hold values from 0.5 to 4
- neighbours: int32 [128, 4], P('elem'), may hold values from -1 to 127, as said below
Outputs:
- solution: float32 [1024, 128, 128], P('mode', 'elem')
Inputs may be any that keep to these rules, and one draw needn't show every extreme that they name: `stiffness`: symmetric with a positive diagonal. `neighbours`: elements lie on a grid of 2 rows, periodic along the rows, and 4 columns a group of 8 elements, groups in order along the columns with walls at both ends. A group's first 2 elements form its first column and its last 2 its last column; a neighbour in another group is in the next or previous group, among its first or last 2 elements.
All inputs are finite; a program needn't handle non-finite values.
Results may differ from a plain program's by a relative error of at most 0.0001.
Values sent between devices are 32-bit elements; how exact they have to be, the bound alone decides.
A program may use at most 128 MiB of HBM per device.

v0:
```python
import functools
import math

import jax
import jax.numpy as jnp
import ml_dtypes
import numpy as np
from jax import lax
from jax.experimental import pallas as pl
from jax.experimental.pallas import tpu as pltpu
from jax.sharding import PartitionSpec as P

dt_step = 0.5
first_weight = 0.7
second_weight = 1.1
CHUNKS = 8
vmem_bytes = 67043328
vmem_spare = 262144
MESH = pl.DeviceIdType.MESH
bf16 = jnp.bfloat16
f32 = jnp.float32


def dft_tables(planes, modes):
    half = planes // 2
    rows = np.arange(planes)
    waves = np.where(rows <= half, rows, rows - half)
    phase = (waves[:, None] * np.arange(half)[None, :]) % planes
    angles = 2.0 * math.pi / planes * phase
    table = np.where((rows <= half)[:, None], np.cos(angles), -np.sin(angles)) * planes ** (-0.5)
    table = table.reshape(modes, planes // modes // 2, 2, half).transpose(0, 2, 1, 3)
    high = table.astype(ml_dtypes.bfloat16)
    low = (table - high.astype(np.float64)).astype(ml_dtypes.bfloat16)
    return np.stack([high, low], axis=2)


def split(values):
    high = values.astype(bf16)
    low = (values - high.astype(f32)).astype(bf16)
    return high, low


def kernel(
    modes, groups, planes, elems, group_elems, rows, nodes,
    vel_hbm, prev_hbm, table_hbm, der_hbm, stiff_hbm, coup_hbm, reac, axial, near,
    outv,
    vel, prev, table, der, stiff, coup, w_slope, w_apply, folded, sent, rhs, first, inverse,
    halo_prev, halo_first, pairs,
    vel_sem, table_sem, prev_sem, small_sem, y_send, y_recv, p_send, p_recv, f_send, f_recv,
):
    half = planes // 2
    rim = group_elems // 4
    count = rows // CHUNKS
    per_parity = CHUNKS // 2
    early = min(rim, elems)
    spans = [(0, early)] + ([(early, elems)] if early < elems else [])
    faces = faces_of(group_elems)
    me = lax.axis_index("mode")
    group = lax.axis_index("elem")
    zero_slot = group_elems + 2 * rim

    def skip(mode):
        return jnp.where(mode < modes // 2, 0, elems - early)

    def element_of(mode, slot):
        if isinstance(mode, int):
            turn = 0 if mode < modes // 2 else elems - early
            return mode * elems + (slot + turn) % elems
        return mode * elems + lax.rem(slot + skip(mode), elems)

    def slot_of(element):
        mode, place = element // elems, element % elems
        turn = 0 if mode < modes // 2 else elems - early
        return mode, (place - turn) % elems

    barrier = pltpu.get_barrier_semaphore()
    for step in range(1, modes):
        pl.semaphore_signal(
            barrier, inc=1, device_id={"mode": lax.rem(me + step, modes)}, device_id_type=MESH
        )
    has_left = group > 0
    has_right = group < groups - 1

    @pl.when(has_left)
    def _():
        pl.semaphore_signal(barrier, inc=1, device_id={"elem": group - 1}, device_id_type=MESH)

    @pl.when(has_right)
    def _():
        pl.semaphore_signal(barrier, inc=1, device_id={"elem": group + 1}, device_id_type=MESH)

    der_load = pltpu.make_async_copy(der_hbm, der, small_sem.at[0])
    stiff_load = pltpu.make_async_copy(stiff_hbm, stiff, small_sem.at[1])
    coup_load = pltpu.make_async_copy(coup_hbm, coup, small_sem.at[2])

    def vel_load(slot):
        return pltpu.make_async_copy(
            vel_hbm.at[:, lax.rem(slot + skip(me), elems)], vel.at[slot], vel_sem.at[slot]
        )

    def table_load(step, parity):
        owner = lax.rem(me + step, modes)
        return pltpu.make_async_copy(
            table_hbm.at[owner, parity], table.at[step, parity], table_sem.at[step, parity]
        )

    def prev_load(parity, e):
        return pltpu.make_async_copy(
            prev_hbm.at[:, parity, e], prev.at[parity, e], prev_sem.at[parity, e]
        )

    steps = [*range(1, modes), 0]
    der_load.start()
    for slot in range(early):
        vel_load(slot).start()
    for parity in range(2):
        for step in range(1, modes):
            table_load(step, parity).start()
    for slot in range(early, elems):
        vel_load(slot).start()
    for parity in range(2):
        table_load(0, parity).start()
    for parity in range(2):
        for e in range(group_elems):
            prev_load(parity, e).start()
    stiff_load.start()
    coup_load.start()

    def halo_copies(source, halo, send, recv, c):
        right = pltpu.make_async_remote_copy(
            source(c, 0), halo.at[0, c], send.at[0, c], recv.at[0, c],
            device_id={"elem": group + 1}, device_id_type=MESH,
        )
        left = pltpu.make_async_remote_copy(
            source(c, 1), halo.at[1, c], send.at[1, c], recv.at[1, c],
            device_id={"elem": group - 1}, device_id_type=MESH,
        )
        return right, left

    def prev_rim(c, side, i):
        parity, place = c // per_parity, c % per_parity
        return pltpu.make_async_remote_copy(
            prev_hbm.at[
                pl.ds(place * count, count), parity, (group_elems - rim) * (1 - side) + i
            ],
            halo_prev.at[side, c, i], p_send.at[side, c, i], p_recv.at[side, c, i],
            device_id={"elem": group + 1 - 2 * side}, device_id_type=MESH,
        )

    def first_copies(c):
        def source(c, side):
            return first.at[c, pl.ds((group_elems - rim) * (1 - side), rim)]

        return halo_copies(source, halo_first, f_send, f_recv, c)

    def start_halo(copies):
        right, left = copies
        pl.when(has_right)(right.start)
        pl.when(has_left)(left.start)

    def wait_halo_recv(copies):
        right, left = copies
        pl.when(has_left)(right.wait_recv)
        pl.when(has_right)(left.wait_recv)

    def wait_halo_send(copies):
        right, left = copies
        pl.when(has_right)(right.wait_send)
        pl.when(has_left)(left.wait_send)

    def each_prev_rim(c, side, act):
        for i in range(rim):
            act(prev_rim(c, side, i))

    pl.semaphore_wait(
        barrier, modes - 1 + has_left.astype(jnp.int32) + has_right.astype(jnp.int32)
    )

    def send_prev(c, carry):
        pl.when(has_right)(lambda: each_prev_rim(c, 0, lambda copy: copy.start()))
        pl.when(has_left)(lambda: each_prev_rim(c, 1, lambda copy: copy.start()))
        return carry

    lax.fori_loop(0, CHUNKS, send_prev, 0)

    def set_weights(ref, at, matrix):
        high, low = split(matrix.T)
        for part in range(2):
            ref[pl.ds(at + part * nodes, nodes), pl.ds(0, nodes)] = high
            ref[pl.ds(at + part * nodes, nodes), pl.ds(nodes, nodes)] = low

    der_load.wait()
    set_weights(w_slope, 0, der[...])

    block = min(256, half)

    def advect(slot):
        vel_load(slot).wait()
        for b in range(half // block):
            lower = vel[slot, pl.ds(b * block, block), :]
            upper = vel[slot, pl.ds(half + b * block, block), :]
            values = jnp.concatenate([lower, upper], axis=0)
            both = jnp.dot(
                jnp.concatenate(split(values), axis=1), w_slope[...], preferred_element_type=f32
            )
            slope = both[:, :nodes] + both[:, nodes:]
            product = values - dt_step * values * slope
            lower, upper = product[:block], product[block:]
            for parity, value in enumerate((lower + upper, lower - upper)):
                high, low = split(value)
                where = (pl.ds(b * block, block), pl.ds(slot * nodes, nodes))
                folded[(parity, 0) + where] = high
                folded[(parity, 1) + where] = low

    def transform(step, parity, start, stop):
        span = pl.ds(start * nodes, (stop - start) * nodes)
        data_high, data_low = folded[parity, 0, :, span], folded[parity, 1, :, span]
        t_high, t_low = table[step, parity, 0], table[step, parity, 1]
        return (
            jnp.dot(t_high, data_high, preferred_element_type=f32)
            + jnp.dot(t_low, data_high, preferred_element_type=f32)
            + jnp.dot(t_high, data_low, preferred_element_type=f32)
        )

    def put_rows(ref, parity, block_rows, start, stop):
        for j in range(per_parity):
            for slot in range(start, stop):
                at = (slot - start) * nodes
                ref[parity * per_parity + j, slot] = block_rows[
                    j * count : (j + 1) * count, at : at + nodes
                ]

    def y_copy(step, c, k):
        start, stop = spans[k]
        return pltpu.make_async_remote_copy(
            sent.at[step - 1, c, pl.ds(start, stop - start)],
            rhs.at[me, c, pl.ds(start, stop - start)],
            y_send.at[k, step - 1, c], y_recv.at[k, step - 1, c],
            device_id={"mode": lax.rem(me + step, modes)}, device_id_type=MESH,
        )

    for k, (start, stop) in enumerate(spans):
        for slot in range(start, stop):
            advect(slot)
        for parity in range(2):
            for step in range(1, modes):
                if k == 0:
                    table_load(step, parity).wait()
                put_rows(sent.at[step - 1], parity, transform(step, parity, start, stop), start, stop)
                for j in range(per_parity):
                    y_copy(step, parity * per_parity + j, k).start()

    for parity in range(2):
        table_load(0, parity).wait()
        put_rows(rhs.at[me], parity, transform(0, parity, 0, elems), 0, elems)

    stiff_load.wait()
    coup_load.wait()
    set_weights(w_apply, 0, stiff[...])
    for f in range(faces):
        matrix = coup[f] + coup[f + 1] if f == faces - 1 and faces < 4 else coup[f]
        set_weights(w_apply, 2 * nodes * (f + 1), matrix)
    eye = lax.broadcasted_iota(jnp.int32, (nodes, nodes), 0) == lax.broadcasted_iota(
        jnp.int32, (nodes, nodes), 1
    )
    diagonal = jnp.sum(jnp.where(eye, stiff[...], 0.0), axis=0, keepdims=True)
    pairs[zero_slot] = jnp.zeros((count, 2 * nodes), bf16)
    for parity in range(2):
        for e in range(group_elems):
            prev_load(parity, e).wait()

    def put_pair(slot, value):
        high, low = split(value)
        pairs[slot, :, pl.ds(0, nodes)] = high
        pairs[slot, :, pl.ds(nodes, nodes)] = low

    def put_halo(halo, c):
        @pl.when(has_left)
        def _():
            for i in range(rim):
                put_pair(i, halo[0, c, i])

        @pl.when(has_right)
        def _():
            for i in range(rim):
                put_pair(rim + group_elems + i, halo[1, c, i])

    def apply():
        columns = [
            jnp.concatenate([pairs[rim + e] for e in range(group_elems)], axis=0)
        ]
        for f in range(faces):
            found = []
            for e in range(group_elems):
                n = near[f, e]
                slot = jnp.clip(n - group * group_elems + rim, 0, zero_slot - 1)
                slot = jnp.where(n >= 0, slot, zero_slot)
                found.append(pairs[slot])
            columns.append(jnp.concatenate(found, axis=0))
        both = jnp.dot(
            jnp.concatenate(columns, axis=1), w_apply[...], preferred_element_type=f32
        )
        return both[:, :nodes] + both[:, nodes:]

    def prev_rows(c, e):
        return prev[c // per_parity, e, pl.ds((c % per_parity) * count, count), :]

    def shifts(c):
        places = lax.broadcasted_iota(jnp.int32, (count, nodes), 0)
        row = me * rows + 2 * ((c % per_parity) * count + places) + c // per_parity
        wave = jnp.where(row <= half, row, row - half).astype(f32)
        return 4.0 * (wave / half) ** 2

    def complete(c, mode, slot, e):
        first[c, e] = first[c, e] + first_weight * inverse[c, e] * rhs[mode, c, slot]

    def first_sweep(c, carry):
        for e in range(group_elems):
            put_pair(rim + e, prev_rows(c, e))
        pl.when(has_left)(lambda: each_prev_rim(c, 0, lambda copy: copy.wait_recv()))
        pl.when(has_right)(lambda: each_prev_rim(c, 1, lambda copy: copy.wait_recv()))
        put_halo(halo_prev, c)
        applied = apply()
        shift = shifts(c)
        for e in range(group_elems):
            scaling = reac[e] + shift * axial[e]
            recip = 1.0 / (diagonal + scaling)
            inverse[c, e] = recip
            value = prev_rows(c, e)
            part = applied[e * count : (e + 1) * count]
            first[c, e] = value - first_weight * recip * (part + scaling * value)
        for slot in range(early, elems):
            complete(c, me, slot, element_of(me, slot))
        for step in range(1, modes):
            y_copy(step, c, 0).wait_recv()
        for mode in range(modes):
            for slot in range(early):
                complete(c, mode, slot, element_of(mode, slot))
        start_halo(first_copies(c))
        return carry

    def second_sweep(c, carry):
        for mode in range(modes):
            for slot in range(early):
                e = element_of(mode, slot)
                put_pair(rim + e, first[c, e])
        for slot in range(early, elems):
            e = element_of(me, slot)
            put_pair(rim + e, first[c, e])
        wait_halo_recv(first_copies(c))
        put_halo(halo_first, c)
        if early < elems:
            for step in range(1, modes):
                y_copy(step, c, 1).wait_recv()
                mode = lax.rem(me + step, modes)
                for slot in range(early, elems):
                    e = element_of(mode, slot)
                    complete(c, mode, slot, e)
                    put_pair(rim + e, first[c, e])
        applied = apply()
        shift = shifts(c)
        for e in range(group_elems):
            mode, slot = slot_of(e)
            scaling = reac[e] + shift * axial[e]
            value = first[c, e]
            part = applied[e * count : (e + 1) * count]
            start = (2 * (c % per_parity) * count + c // per_parity) * group_elems + e
            outv[pl.ds(start, count, stride=2 * group_elems), :] = value + second_weight * inverse[
                c, e
            ] * (rhs[mode, c, slot] - (part + scaling * value))
        return carry

    lax.fori_loop(0, CHUNKS, first_sweep, 0)
    lax.fori_loop(0, CHUNKS, second_sweep, 0)

    def finish(c, carry):
        pl.when(has_right)(lambda: each_prev_rim(c, 0, lambda copy: copy.wait_send()))
        pl.when(has_left)(lambda: each_prev_rim(c, 1, lambda copy: copy.wait_send()))
        wait_halo_send(first_copies(c))
        for k in range(len(spans)):
            for step in range(1, modes):
                y_copy(step, c, k).wait_send()
        return carry

    lax.fori_loop(0, CHUNKS, finish, 0)


def faces_of(group_elems):
    return 3 if group_elems // 4 == 2 else 4


def body(modes, groups, velocity, previous, derivative, stiffness, coupling, reaction, axial_weight, neighbours):
    planes, elems, nodes = velocity.shape
    rows, group_elems, _ = previous.shape
    half = planes // 2
    rim = group_elems // 4
    count = rows // CHUNKS
    tables = jnp.asarray(dft_tables(planes, modes))
    run = functools.partial(kernel, modes, groups, planes, elems, group_elems, rows, nodes)
    anywhere = pl.BlockSpec(memory_space=pltpu.HBM)
    scalar = pl.BlockSpec(memory_space=pltpu.SMEM)
    dma = pltpu.SemaphoreType.DMA
    taps = faces_of(group_elems) + 1
    scratch = [
        pltpu.VMEM((elems, planes, nodes), f32),
        pltpu.VMEM((2, group_elems, rows // 2, nodes), f32),
        pltpu.VMEM(tables.shape, bf16),
        pltpu.VMEM((nodes, nodes), f32),
        pltpu.VMEM((nodes, nodes), f32),
        pltpu.VMEM((4, nodes, nodes), f32),
        pltpu.VMEM((2 * nodes, 2 * nodes), bf16),
        pltpu.VMEM((taps * 2 * nodes, 2 * nodes), bf16),
        pltpu.VMEM((2, 2, half, elems * nodes), bf16),
        pltpu.VMEM((modes - 1, CHUNKS, elems, count, nodes), f32),
        pltpu.VMEM((modes, CHUNKS, elems, count, nodes), f32),
        pltpu.VMEM((CHUNKS, group_elems, count, nodes), f32),
        pltpu.VMEM((CHUNKS, group_elems, count, nodes), f32),
        pltpu.VMEM((2, CHUNKS, rim, count, nodes), f32),
        pltpu.VMEM((2, CHUNKS, rim, count, nodes), f32),
        pltpu.VMEM((group_elems + 2 * rim + 1, count, 2 * nodes), bf16),
    ]
    semaphores = [
        dma((elems,)),
        dma((modes, 2)),
        dma((2, group_elems)),
        dma((3,)),
        dma((2, modes - 1, CHUNKS)),
        dma((2, modes - 1, CHUNKS)),
        dma((2, CHUNKS, rim)),
        dma((2, CHUNKS, rim)),
        dma((2, CHUNKS)),
        dma((2, CHUNKS)),
    ]
    out = pl.pallas_call(
        run,
        out_shape=pltpu.VMEM((rows * group_elems, nodes), f32),
        in_specs=[anywhere] * 6 + [scalar] * 3,
        out_specs=pl.BlockSpec(memory_space=pltpu.VMEM),
        scratch_shapes=scratch + semaphores,
        compiler_params=pltpu.CompilerParams(
            collective_id=0, has_side_effects=True, vmem_limit_bytes=vmem_bytes - 4 * rows * group_elems * nodes - vmem_spare
        ),
        name="advect_helmholtz",
    )(
        velocity,
        previous.reshape(rows // 2, 2, group_elems, nodes),
        tables,
        derivative,
        stiffness,
        coupling,
        reaction,
        axial_weight,
        neighbours.T,
    )
    return out.reshape(rows, group_elems, nodes)


def solution(mesh):
    return jax.shard_map(
        functools.partial(body, mesh.shape["mode"], mesh.shape["elem"]),
        mesh=mesh,
        in_specs=(
            P(None, ("elem", "mode"), None),
            P("mode", "elem", None),
            P(),
            P(),
            P(),
            P("elem"),
            P("elem"),
            P("elem", None),
        ),
        out_specs=P("mode", "elem", None),
        check_vma=False,
    )
```

profile of v0, /device:TPU:0, one launch (start us, length us, event | category | flops | bytes accessed | tf_op | source)
XLA Modules:
  0.0 33.6 jit_solution(11141827283055166345)
XLA Ops:
  0.0 32.3 %advect_helmholtz.1 = f32[4096,128]{1,0:T(8,128)S(1)} custom-call(f32[1024,4,128]{2,1,0:T(4,128)} %vel_hbm.1, f32[256,2,8,128]{3,2,1,0:T(8,128)} %bitcast.4, bf16[2,2,2,256,512]{4,3,2,1,0:T(8,128)(2,1)} %constant.2.clone.table_hbm, f32[128,128]{1,0:T(8,128)} %der_hbm.1, f32[128,128]{1,0:T(8,128)} %stiff_hbm.1, f32[4,128,128]{2,1,0:T(8,128)} %coup_hbm.1, ...), custom_call_target="tpu_custom_call" | custom-call | tf_op jit(solution)/shard_map/advect_helmholtz/pallas_call | solution.py:434
  32.3 1.3 %copy.11 = f32[512,8,128]{2,1,0:T(8,128)} copy(f32[512,8,128]{2,1,0:T(8,128)S(1)} %bitcast.3) | data formatting | bytes 4194304
where the time goes:
time: 33.8 us; the launch traced here: 33.6 us
  Pallas kernels  32.3 us (96%)
  local copies, waits for them, and re-layouts  1.32 us (4%)
    pallas_call x1, Pallas kernels, body(): pl.pallas_call(run, out_shape=pltpu.VMEM((rows * group_elems, nodes), f32...  32.3 us
    unnamed x1, local copies, waits for them, and re-layouts  1.32 us

commit v1 on v0

--- a/solution.py
+++ b/solution.py
@@ -14,6 +14,7 @@
 first_weight = 0.7
 second_weight = 1.1
 CHUNKS = 8
+PIECES = (((0, 1), (1, 4), (4, 8)), ((0, 4), (4, 6), (6, 7), (7, 8)))
 vmem_bytes = 67043328
 vmem_spare = 262144
 MESH = pl.DeviceIdType.MESH
@@ -42,10 +43,10 @@
 
 def kernel(
     modes, groups, planes, elems, group_elems, rows, nodes,
-    vel_hbm, prev_hbm, table_hbm, der_hbm, stiff_hbm, coup_hbm, reac, axial, near,
+    vel_hbm, prev_hbm, table_hbm, der_hbm, stiff_hbm, coup_hbm, reac_hbm, axial_hbm, near_hbm,
     outv,
     vel, prev, table, der, stiff, coup, w_slope, w_apply, folded, sent, rhs, first, inverse,
-    halo_prev, halo_first, pairs,
+    halo_prev, halo_first, pairs, reac, axial, near,
     vel_sem, table_sem, prev_sem, small_sem, y_send, y_recv, p_send, p_recv, f_send, f_recv,
 ):
     half = planes // 2
@@ -93,6 +94,11 @@
     stiff_load = pltpu.make_async_copy(stiff_hbm, stiff, small_sem.at[1])
     coup_load = pltpu.make_async_copy(coup_hbm, coup, small_sem.at[2])
 
+    scalar_loads = [
+        pltpu.make_async_copy(src, dst, small_sem.at[3 + i])
+        for i, (src, dst) in enumerate([(reac_hbm, reac), (axial_hbm, axial), (near_hbm, near)])
+    ]
+
     def vel_load(slot):
         return pltpu.make_async_copy(
             vel_hbm.at[:, lax.rem(slot + skip(me), elems)], vel.at[slot], vel_sem.at[slot]
@@ -125,6 +131,8 @@
             prev_load(parity, e).start()
     stiff_load.start()
     coup_load.start()
+    for load in scalar_loads:
+        load.start()
 
     def halo_copies(source, halo, send, recv, c):
         right = pltpu.make_async_remote_copy(
@@ -137,13 +145,10 @@
         )
         return right, left
 
-    def prev_rim(c, side, i):
-        parity, place = c // per_parity, c % per_parity
+    def prev_rim(parity, side, i):
         return pltpu.make_async_remote_copy(
-            prev_hbm.at[
-                pl.ds(place * count, count), parity, (group_elems - rim) * (1 - side) + i
-            ],
-            halo_prev.at[side, c, i], p_send.at[side, c, i], p_recv.at[side, c, i],
+            prev_hbm.at[:, parity, (group_elems - rim) * (1 - side) + i],
+            halo_prev.at[side, parity, i], p_send.at[side, parity, i], p_recv.at[side, parity, i],
             device_id={"elem": group + 1 - 2 * side}, device_id_type=MESH,
         )
 
@@ -168,20 +173,18 @@
         pl.when(has_right)(right.wait_send)
         pl.when(has_left)(left.wait_send)
 
-    def each_prev_rim(c, side, act):
+    def each_prev_rim(parity, act_right, act_left):
         for i in range(rim):
-            act(prev_rim(c, side, i))
+            right, left = prev_rim(parity, 0, i), prev_rim(parity, 1, i)
+            pl.when(act_right[0])(getattr(right, act_right[1]))
+            pl.when(act_left[0])(getattr(left, act_left[1]))
 
     pl.semaphore_wait(
         barrier, modes - 1 + has_left.astype(jnp.int32) + has_right.astype(jnp.int32)
     )
 
-    def send_prev(c, carry):
-        pl.when(has_right)(lambda: each_prev_rim(c, 0, lambda copy: copy.start()))
-        pl.when(has_left)(lambda: each_prev_rim(c, 1, lambda copy: copy.start()))
-        return carry
-
-    lax.fori_loop(0, CHUNKS, send_prev, 0)
+    for parity in range(2):
+        each_prev_rim(parity, (has_right, "start"), (has_left, "start"))
 
     def set_weights(ref, at, matrix):
         high, low = split(matrix.T)
@@ -212,32 +215,40 @@
                 folded[(parity, 0) + where] = high
                 folded[(parity, 1) + where] = low
 
-    def transform(step, parity, start, stop):
+    def transform(step, parity, start, stop, at=0, size=rows // 2):
         span = pl.ds(start * nodes, (stop - start) * nodes)
         data_high, data_low = folded[parity, 0, :, span], folded[parity, 1, :, span]
-        t_high, t_low = table[step, parity, 0], table[step, parity, 1]
+        t_high = table[step, parity, 0, pl.ds(at, size), :]
+        t_low = table[step, parity, 1, pl.ds(at, size), :]
         return (
             jnp.dot(t_high, data_high, preferred_element_type=f32)
             + jnp.dot(t_low, data_high, preferred_element_type=f32)
             + jnp.dot(t_high, data_low, preferred_element_type=f32)
         )
 
-    def put_rows(ref, parity, block_rows, start, stop):
-        for j in range(per_parity):
+    def put_rows(ref, parity, block_rows, start, stop, first_j=0):
+        for j in range(block_rows.shape[0] // count):
             for slot in range(start, stop):
                 at = (slot - start) * nodes
-                ref[parity * per_parity + j, slot] = block_rows[
+                ref[parity * per_parity + first_j + j, slot] = block_rows[
                     j * count : (j + 1) * count, at : at + nodes
                 ]
 
-    def y_copy(step, c, k):
-        start, stop = spans[k]
+    def y_copy(step, k, n):
+        (start, stop), (at, end) = spans[k], PIECES[k][n]
+        where = (pl.ds(at, end - at), pl.ds(start, stop - start))
         return pltpu.make_async_remote_copy(
-            sent.at[step - 1, c, pl.ds(start, stop - start)],
-            rhs.at[me, c, pl.ds(start, stop - start)],
-            y_send.at[k, step - 1, c], y_recv.at[k, step - 1, c],
+            sent.at[(step - 1,) + where], rhs.at[(me,) + where],
+            y_send.at[k, step - 1, n], y_recv.at[k, step - 1, n],
             device_id={"mode": lax.rem(me + step, modes)}, device_id_type=MESH,
         )
+
+    def wait_pieces(k, c):
+        for n, (at, _) in enumerate(PIECES[k]):
+            @pl.when(c == at)
+            def _():
+                for step in range(1, modes):
+                    y_copy(step, k, n).wait_recv()
 
     for k, (start, stop) in enumerate(spans):
         for slot in range(start, stop):
@@ -246,9 +257,13 @@
             for step in range(1, modes):
                 if k == 0:
                     table_load(step, parity).wait()
-                put_rows(sent.at[step - 1], parity, transform(step, parity, start, stop), start, stop)
-                for j in range(per_parity):
-                    y_copy(step, parity * per_parity + j, k).start()
+                cuts = [0, 1, per_parity] if k == 0 and parity == 0 else [0, per_parity]
+                for j, stop_j in zip(cuts, cuts[1:]):
+                    part = transform(step, parity, start, stop, j * count, (stop_j - j) * count)
+                    put_rows(sent.at[step - 1], parity, part, start, stop, j)
+                    for n, (_, end) in enumerate(PIECES[k]):
+                        if parity * per_parity + j < end <= parity * per_parity + stop_j:
+                            y_copy(step, k, n).start()
 
     for parity in range(2):
         table_load(0, parity).wait()
@@ -256,6 +271,8 @@
 
     stiff_load.wait()
     coup_load.wait()
+    for load in scalar_loads:
+        load.wait()
     set_weights(w_apply, 0, stiff[...])
     for f in range(faces):
         matrix = coup[f] + coup[f + 1] if f == faces - 1 and faces < 4 else coup[f]
@@ -278,12 +295,12 @@
         @pl.when(has_left)
         def _():
             for i in range(rim):
-                put_pair(i, halo[0, c, i])
+                put_pair(i, halo(0, c, i))
 
         @pl.when(has_right)
         def _():
             for i in range(rim):
-                put_pair(rim + group_elems + i, halo[1, c, i])
+                put_pair(rim + group_elems + i, halo(1, c, i))
 
     def apply():
         columns = [
@@ -305,6 +322,9 @@
     def prev_rows(c, e):
         return prev[c // per_parity, e, pl.ds((c % per_parity) * count, count), :]
 
+    def prev_halo_rows(side, c, i):
+        return halo_prev[side, c // per_parity, i, pl.ds((c % per_parity) * count, count), :]
+
     def shifts(c):
         places = lax.broadcasted_iota(jnp.int32, (count, nodes), 0)
         row = me * rows + 2 * ((c % per_parity) * count + places) + c // per_parity
@@ -317,9 +337,11 @@
     def first_sweep(c, carry):
         for e in range(group_elems):
             put_pair(rim + e, prev_rows(c, e))
-        pl.when(has_left)(lambda: each_prev_rim(c, 0, lambda copy: copy.wait_recv()))
-        pl.when(has_right)(lambda: each_prev_rim(c, 1, lambda copy: copy.wait_recv()))
-        put_halo(halo_prev, c)
+        for parity in range(2):
+            pl.when(c == parity * per_parity)(
+                lambda: each_prev_rim(parity, (has_left, "wait_recv"), (has_right, "wait_recv"))
+            )
+        put_halo(prev_halo_rows, c)
         applied = apply()
         shift = shifts(c)
         for e in range(group_elems):
@@ -331,8 +353,7 @@
             first[c, e] = value - first_weight * recip * (part + scaling * value)
         for slot in range(early, elems):
             complete(c, me, slot, element_of(me, slot))
-        for step in range(1, modes):
-            y_copy(step, c, 0).wait_recv()
+        wait_pieces(0, c)
         for mode in range(modes):
             for slot in range(early):
                 complete(c, mode, slot, element_of(mode, slot))
@@ -348,10 +369,10 @@
             e = element_of(me, slot)
             put_pair(rim + e, first[c, e])
         wait_halo_recv(first_copies(c))
-        put_halo(halo_first, c)
+        put_halo(lambda side, c, i: halo_first[side, c, i], c)
         if early < elems:
+            wait_pieces(1, c)
             for step in range(1, modes):
-                y_copy(step, c, 1).wait_recv()
                 mode = lax.rem(me + step, modes)
                 for slot in range(early, elems):
                     e = element_of(mode, slot)
@@ -374,15 +395,16 @@
     lax.fori_loop(0, CHUNKS, second_sweep, 0)
 
     def finish(c, carry):
-        pl.when(has_right)(lambda: each_prev_rim(c, 0, lambda copy: copy.wait_send()))
-        pl.when(has_left)(lambda: each_prev_rim(c, 1, lambda copy: copy.wait_send()))
         wait_halo_send(first_copies(c))
-        for k in range(len(spans)):
+        return carry
+
+    lax.fori_loop(0, CHUNKS, finish, 0)
+    for parity in range(2):
+        each_prev_rim(parity, (has_right, "wait_send"), (has_left, "wait_send"))
+    for k in range(len(spans)):
+        for n in range(len(PIECES[k])):
             for step in range(1, modes):
-                y_copy(step, c, k).wait_send()
-        return carry
-
-    lax.fori_loop(0, CHUNKS, finish, 0)
+                y_copy(step, k, n).wait_send()
 
 
 def faces_of(group_elems):
@@ -398,7 +420,6 @@
     tables = jnp.asarray(dft_tables(planes, modes))
     run = functools.partial(kernel, modes, groups, planes, elems, group_elems, rows, nodes)
     anywhere = pl.BlockSpec(memory_space=pltpu.HBM)
-    scalar = pl.BlockSpec(memory_space=pltpu.SMEM)
     dma = pltpu.SemaphoreType.DMA
     taps = faces_of(group_elems) + 1
     scratch = [
@@ -415,26 +436,29 @@
         pltpu.VMEM((modes, CHUNKS, elems, count, nodes), f32),
         pltpu.VMEM((CHUNKS, group_elems, count, nodes), f32),
         pltpu.VMEM((CHUNKS, group_elems, count, nodes), f32),
-        pltpu.VMEM((2, CHUNKS, rim, count, nodes), f32),
+        pltpu.VMEM((2, 2, rim, rows // 2, nodes), f32),
         pltpu.VMEM((2, CHUNKS, rim, count, nodes), f32),
         pltpu.VMEM((group_elems + 2 * rim + 1, count, 2 * nodes), bf16),
+        pltpu.SMEM((group_elems,), f32),
+        pltpu.SMEM((group_elems,), f32),
+        pltpu.SMEM((4, group_elems), jnp.int32),
     ]
     semaphores = [
         dma((elems,)),
         dma((modes, 2)),
         dma((2, group_elems)),
-        dma((3,)),
+        dma((6,)),
         dma((2, modes - 1, CHUNKS)),
         dma((2, modes - 1, CHUNKS)),
-        dma((2, CHUNKS, rim)),
-        dma((2, CHUNKS, rim)),
+        dma((2, 2, rim)),
+        dma((2, 2, rim)),
         dma((2, CHUNKS)),
         dma((2, CHUNKS)),
     ]
     out = pl.pallas_call(
         run,
         out_shape=pltpu.VMEM((rows * group_elems, nodes), f32),
-        in_specs=[anywhere] * 6 + [scalar] * 3,
+        in_specs=[anywhere] * 9,
         out_specs=pl.BlockSpec(memory_space=pltpu.VMEM),
         scratch_shapes=scratch + semaphores,
         compiler_params=pltpu.CompilerParams(

time: 33.8 us -> 32.2 us (0.953)
  Pallas kernels: 32.3 us -> 30.7 us
    pallas_call x1, Pallas kernels: 32.3 us -> 30.7 us  [body(): pl.pallas_call(run, out_shape=pltpu.VMEM((rows * group_elems, nodes), f32...]
where the time goes in v1:
time: 32.2 us; the launch traced here: 32.1 us
  Pallas kernels  30.7 us (95%)
  local copies, waits for them, and re-layouts  1.32 us (4%)
    pallas_call x1, Pallas kernels, body(): pl.pallas_call(run, out_shape=pltpu.VMEM((rows * group_elems, nodes), f32...  30.7 us
    unnamed x1, local copies, waits for them, and re-layouts  1.32 us

profile of v1, /device:TPU:0, one launch (start us, length us, event | category | flops | bytes accessed | tf_op | source)
XLA Modules:
  0.0 32.1 jit_solution(4363556099230096323)
XLA Ops:
  0.0 30.7 %advect_helmholtz.1 = f32[4096,128]{1,0:T(8,128)S(1)} custom-call(f32[1024,4,128]{2,1,0:T(4,128)} %vel_hbm.1, f32[256,2,8,128]{3,2,1,0:T(8,128)} %bitcast.4, bf16[2,2,2,256,512]{4,3,2,1,0:T(8,128)(2,1)} %constant.2.clone.table_hbm, f32[128,128]{1,0:T(8,128)} %der_hbm.1, f32[128,128]{1,0:T(8,128)} %stiff_hbm.1, f32[4,128,128]{2,1,0:T(8,128)} %coup_hbm.1, ...), custom_call_target="tpu_custom_call" | custom-call | tf_op jit(solution)/shard_map/advect_helmholtz/pallas_call | solution.py:458
  30.7 1.3 %copy.11 = f32[512,8,128]{2,1,0:T(8,128)} copy(f32[512,8,128]{2,1,0:T(8,128)S(1)} %bitcast.3) | data formatting | bytes 4194304

commit v2 on v1

--- a/solution.py
+++ b/solution.py
@@ -14,7 +14,10 @@
 first_weight = 0.7
 second_weight = 1.1
 CHUNKS = 8
-PIECES = (((0, 1), (1, 4), (4, 8)), ((0, 4), (4, 6), (6, 7), (7, 8)))
+LEAD_CUTS = (0, 1, 4, 8)
+EARLY_CUTS = (0, 4, 8)
+REST_AT = 0
+LATE_CUTS = (0, 4, 6, 7, 8)
 vmem_bytes = 67043328
 vmem_spare = 262144
 MESH = pl.DeviceIdType.MESH
@@ -47,14 +50,20 @@
     outv,
     vel, prev, table, der, stiff, coup, w_slope, w_apply, folded, sent, rhs, first, inverse,
     halo_prev, halo_first, pairs, reac, axial, near,
-    vel_sem, table_sem, prev_sem, small_sem, y_send, y_recv, p_send, p_recv, f_send, f_recv,
+    lead_sem, vel_sem, table_sem, prev_sem, small_sem, y_send, y_recv, p_send, p_recv, f_send, f_recv,
 ):
     half = planes // 2
     rim = group_elems // 4
     count = rows // CHUNKS
     per_parity = CHUNKS // 2
     early = min(rim, elems)
-    spans = [(0, early)] + ([(early, elems)] if early < elems else [])
+    spans = [
+        (start, stop, cuts)
+        for start, stop, cuts in [
+            (0, 1, LEAD_CUTS), (1, early, EARLY_CUTS), (early, elems, LATE_CUTS)
+        ]
+        if start < stop
+    ]
     faces = faces_of(group_elems)
     me = lax.axis_index("mode")
     group = lax.axis_index("elem")
@@ -74,6 +83,63 @@
         turn = 0 if mode < modes // 2 else elems - early
         return mode, (place - turn) % elems
 
+    der_load = pltpu.make_async_copy(der_hbm, der, small_sem.at[0])
+    stiff_load = pltpu.make_async_copy(stiff_hbm, stiff, small_sem.at[1])
+    coup_load = pltpu.make_async_copy(coup_hbm, coup, small_sem.at[2])
+
+    scalar_loads = [
+        pltpu.make_async_copy(src, dst, small_sem.at[3 + i])
+        for i, (src, dst) in enumerate([(reac_hbm, reac), (axial_hbm, axial), (near_hbm, near)])
+    ]
+
+    block = min(256, half)
+
+    def vel_load(slot):
+        return pltpu.make_async_copy(
+            vel_hbm.at[:, lax.rem(slot + skip(me), elems)], vel.at[slot], vel_sem.at[slot]
+        )
+
+    def lead_load(b, side):
+        where = pl.ds(side * half + b * block, block)
+        return pltpu.make_async_copy(
+            vel_hbm.at[where, skip(me)], vel.at[0, where], lead_sem.at[b, side]
+        )
+
+    def table_load(step, parity):
+        owner = lax.rem(me + step, modes)
+        return pltpu.make_async_copy(
+            table_hbm.at[owner, parity], table.at[step, parity], table_sem.at[step, parity]
+        )
+
+    def prev_load(parity, e):
+        return pltpu.make_async_copy(
+            prev_hbm.at[:, parity, e], prev.at[parity, e], prev_sem.at[parity, e]
+        )
+
+    steps = [*range(1, modes), 0]
+    der_load.start()
+    for b in range(half // block):
+        for side in range(2):
+            lead_load(b, side).start()
+    for step in range(1, modes):
+        table_load(step, 0).start()
+    for slot in range(1, early):
+        vel_load(slot).start()
+    for step in range(1, modes):
+        table_load(step, 1).start()
+    def start_rest():
+        for slot in range(early, elems):
+            vel_load(slot).start()
+        for parity in range(2):
+            table_load(0, parity).start()
+        for parity in range(2):
+            for e in range(group_elems):
+                prev_load(parity, e).start()
+        stiff_load.start()
+        coup_load.start()
+        for load in scalar_loads:
+            load.start()
+
     barrier = pltpu.get_barrier_semaphore()
     for step in range(1, modes):
         pl.semaphore_signal(
@@ -89,50 +155,6 @@
     @pl.when(has_right)
     def _():
         pl.semaphore_signal(barrier, inc=1, device_id={"elem": group + 1}, device_id_type=MESH)
-
-    der_load = pltpu.make_async_copy(der_hbm, der, small_sem.at[0])
-    stiff_load = pltpu.make_async_copy(stiff_hbm, stiff, small_sem.at[1])
-    coup_load = pltpu.make_async_copy(coup_hbm, coup, small_sem.at[2])
-
-    scalar_loads = [
-        pltpu.make_async_copy(src, dst, small_sem.at[3 + i])
-        for i, (src, dst) in enumerate([(reac_hbm, reac), (axial_hbm, axial), (near_hbm, near)])
-    ]
-
-    def vel_load(slot):
-        return pltpu.make_async_copy(
-            vel_hbm.at[:, lax.rem(slot + skip(me), elems)], vel.at[slot], vel_sem.at[slot]
-        )
-
-    def table_load(step, parity):
-        owner = lax.rem(me + step, modes)
-        return pltpu.make_async_copy(
-            table_hbm.at[owner, parity], table.at[step, parity], table_sem.at[step, parity]
-        )
-
-    def prev_load(parity, e):
-        return pltpu.make_async_copy(
-            prev_hbm.at[:, parity, e], prev.at[parity, e], prev_sem.at[parity, e]
-        )
-
-    steps = [*range(1, modes), 0]
-    der_load.start()
-    for slot in range(early):
-        vel_load(slot).start()
-    for parity in range(2):
-        for step in range(1, modes):
-            table_load(step, parity).start()
-    for slot in range(early, elems):
-        vel_load(slot).start()
-    for parity in range(2):
-        table_load(0, parity).start()
-    for parity in range(2):
-        for e in range(group_elems):
-            prev_load(parity, e).start()
-    stiff_load.start()
-    coup_load.start()
-    for load in scalar_loads:
-        load.start()
 
     def halo_copies(source, halo, send, recv, c):
         right = pltpu.make_async_remote_copy(
@@ -158,11 +180,6 @@
 
         return halo_copies(source, halo_first, f_send, f_recv, c)
 
-    def start_halo(copies):
-        right, left = copies
-        pl.when(has_right)(right.start)
-        pl.when(has_left)(left.start)
-
     def wait_halo_recv(copies):
         right, left = copies
         pl.when(has_left)(right.wait_recv)
@@ -179,12 +196,13 @@
             pl.when(act_right[0])(getattr(right, act_right[1]))
             pl.when(act_left[0])(getattr(left, act_left[1]))
 
-    pl.semaphore_wait(
-        barrier, modes - 1 + has_left.astype(jnp.int32) + has_right.astype(jnp.int32)
-    )
-
-    for parity in range(2):
-        each_prev_rim(parity, (has_right, "start"), (has_left, "start"))
+    far_right = jnp.logical_and(has_right, lax.rem(group, 4) == 3)
+    far_left = jnp.logical_and(has_left, lax.rem(group, 4) == 0)
+    near_right = jnp.logical_and(has_right, lax.rem(group, 4) != 3)
+    near_left = jnp.logical_and(has_left, lax.rem(group, 4) != 0)
+    left_local = me == 0
+    right_local = me == modes - 1
+    held_back = lax.rem(group, 2) == 1
 
     def set_weights(ref, at, matrix):
         high, low = split(matrix.T)
@@ -195,11 +213,13 @@
     der_load.wait()
     set_weights(w_slope, 0, der[...])
 
-    block = min(256, half)
-
     def advect(slot):
-        vel_load(slot).wait()
+        if slot > 0:
+            vel_load(slot).wait()
         for b in range(half // block):
+            if slot == 0:
+                lead_load(b, 0).wait()
+                lead_load(b, 1).wait()
             lower = vel[slot, pl.ds(b * block, block), :]
             upper = vel[slot, pl.ds(half + b * block, block), :]
             values = jnp.concatenate([lower, upper], axis=0)
@@ -235,36 +255,63 @@
                 ]
 
     def y_copy(step, k, n):
-        (start, stop), (at, end) = spans[k], PIECES[k][n]
-        where = (pl.ds(at, end - at), pl.ds(start, stop - start))
+        start, stop, cuts = spans[k]
+        where = (pl.ds(cuts[n], cuts[n + 1] - cuts[n]), pl.ds(start, stop - start))
         return pltpu.make_async_remote_copy(
             sent.at[(step - 1,) + where], rhs.at[(me,) + where],
             y_send.at[k, step - 1, n], y_recv.at[k, step - 1, n],
             device_id={"mode": lax.rem(me + step, modes)}, device_id_type=MESH,
         )
 
-    def wait_pieces(k, c):
-        for n, (at, _) in enumerate(PIECES[k]):
-            @pl.when(c == at)
-            def _():
+    def start_pieces(k, at=0, end=CHUNKS):
+        for n, cut in enumerate(spans[k][2][1:]):
+            if at < cut <= end:
                 for step in range(1, modes):
-                    y_copy(step, k, n).wait_recv()
-
-    for k, (start, stop) in enumerate(spans):
+                    y_copy(step, k, n).start()
+
+    def wait_pieces(late, c, begin=0, end=CHUNKS, also=True):
+        for at in range(begin, end):
+            due = [
+                (k, n)
+                for k, (start, _, cuts) in enumerate(spans)
+                for n, cut in enumerate(cuts[:-1])
+                if cut == at and (start >= early) == late
+            ]
+            if due:
+                @pl.when(jnp.logical_and(c == at, also))
+                def _():
+                    for k, n in due:
+                        for step in range(1, modes):
+                            y_copy(step, k, n).wait_recv()
+
+    for k, (start, stop, _) in enumerate(spans):
         for slot in range(start, stop):
             advect(slot)
+        if k == 0:
+            pl.semaphore_wait(
+                barrier, modes - 1 + has_left.astype(jnp.int32) + has_right.astype(jnp.int32)
+            )
+
+            each_prev_rim(0, (has_right, "start"), (has_left, "start"))
+            each_prev_rim(1, (near_right, "start"), (near_left, "start"))
         for parity in range(2):
-            for step in range(1, modes):
-                if k == 0:
+            if k == 0:
+                for step in range(1, modes):
                     table_load(step, parity).wait()
-                cuts = [0, 1, per_parity] if k == 0 and parity == 0 else [0, per_parity]
-                for j, stop_j in zip(cuts, cuts[1:]):
+            cuts = [0, 1, per_parity] if k == 0 and parity == 0 else [0, per_parity]
+            for j, stop_j in zip(cuts, cuts[1:]):
+                for step in range(1, modes):
                     part = transform(step, parity, start, stop, j * count, (stop_j - j) * count)
                     put_rows(sent.at[step - 1], parity, part, start, stop, j)
-                    for n, (_, end) in enumerate(PIECES[k]):
-                        if parity * per_parity + j < end <= parity * per_parity + stop_j:
-                            y_copy(step, k, n).start()
-
+                at, end = parity * per_parity + j, parity * per_parity + stop_j
+                if start < early:
+                    start_pieces(k, at, end)
+                else:
+                    pl.when(jnp.logical_not(held_back))(lambda: start_pieces(k, at, end))
+                if k == 0 and at == REST_AT:
+                    start_rest()
+
+    each_prev_rim(1, (far_right, "start"), (far_left, "start"))
     for parity in range(2):
         table_load(0, parity).wait()
         put_rows(rhs.at[me], parity, transform(0, parity, 0, elems), 0, elems)
@@ -351,13 +398,36 @@
             value = prev_rows(c, e)
             part = applied[e * count : (e + 1) * count]
             first[c, e] = value - first_weight * recip * (part + scaling * value)
-        for slot in range(early, elems):
+        for slot in range(elems):
             complete(c, me, slot, element_of(me, slot))
-        wait_pieces(0, c)
-        for mode in range(modes):
+        right, left = first_copies(c)
+        pl.when(jnp.logical_and(has_right, right_local))(right.start)
+        pl.when(jnp.logical_and(has_left, left_local))(left.start)
+        return carry
+
+    def finish_rims(c, carry):
+        wait_pieces(False, c, 0, per_parity)
+        wait_pieces(False, c, per_parity, CHUNKS, jnp.logical_not(held_back))
+        for step in range(1, modes):
+            mode = lax.rem(me + step, modes)
             for slot in range(early):
                 complete(c, mode, slot, element_of(mode, slot))
-        start_halo(first_copies(c))
+        right, left = first_copies(c)
+        pl.when(jnp.logical_and(has_right, jnp.logical_not(right_local)))(right.start)
+        pl.when(jnp.logical_and(has_left, jnp.logical_not(left_local)))(left.start)
+        return carry
+
+    def first_half(parity, carry):
+        at = parity * per_parity
+        lax.fori_loop(at, at + per_parity, first_sweep, 0)
+        lax.fori_loop(at, at + per_parity, finish_rims, 0)
+
+        @pl.when(jnp.logical_and(held_back, parity == 0))
+        def _():
+            wait_pieces(False, per_parity)
+            if early < elems:
+                start_pieces(len(spans) - 1)
+
         return carry
 
     def second_sweep(c, carry):
@@ -371,7 +441,7 @@
         wait_halo_recv(first_copies(c))
         put_halo(lambda side, c, i: halo_first[side, c, i], c)
         if early < elems:
-            wait_pieces(1, c)
+            wait_pieces(True, c)
             for step in range(1, modes):
                 mode = lax.rem(me + step, modes)
                 for slot in range(early, elems):
@@ -391,7 +461,7 @@
             ] * (rhs[mode, c, slot] - (part + scaling * value))
         return carry
 
-    lax.fori_loop(0, CHUNKS, first_sweep, 0)
+    lax.fori_loop(0, 2, first_half, 0)
     lax.fori_loop(0, CHUNKS, second_sweep, 0)
 
     def finish(c, carry):
@@ -402,7 +472,7 @@
     for parity in range(2):
         each_prev_rim(parity, (has_right, "wait_send"), (has_left, "wait_send"))
     for k in range(len(spans)):
-        for n in range(len(PIECES[k])):
+        for n in range(len(spans[k][2]) - 1):
             for step in range(1, modes):
                 y_copy(step, k, n).wait_send()
 
@@ -444,12 +514,13 @@
         pltpu.SMEM((4, group_elems), jnp.int32),
     ]
     semaphores = [
+        dma((half // min(256, half), 2)),
         dma((elems,)),
         dma((modes, 2)),
         dma((2, group_elems)),
         dma((6,)),
-        dma((2, modes - 1, CHUNKS)),
-        dma((2, modes - 1, CHUNKS)),
+        dma((3, modes - 1, CHUNKS)),
+        dma((3, modes - 1, CHUNKS)),
         dma((2, 2, rim)),
         dma((2, 2, rim)),
         dma((2, CHUNKS)),

time: 32.2 us -> 31.1 us (0.966)
  Pallas kernels: 30.7 us -> 29.4 us
    pallas_call x1, Pallas kernels: 30.7 us -> 29.4 us  [body(): pl.pallas_call(run, out_shape=pltpu.VMEM((rows * group_elems, nodes), f32...]
where the time goes in v2:
time: 31.1 us; the launch traced here: 30.8 us
  Pallas kernels  29.4 us (95%)
  local copies, waits for them, and re-layouts  1.32 us (4%)
    pallas_call x1, Pallas kernels, body(): pl.pallas_call(run, out_shape=pltpu.VMEM((rows * group_elems, nodes), f32...  29.4 us
    unnamed x1, local copies, waits for them, and re-layouts  1.32 us

profile of v2, /device:TPU:0, one launch (start us, length us, event | category | flops | bytes accessed | tf_op | source)
XLA Modules:
  0.0 30.8 jit_solution(17162987462578591947)
XLA Ops:
  0.0 29.4 %advect_helmholtz.1 = f32[4096,128]{1,0:T(8,128)S(1)} custom-call(f32[1024,4,128]{2,1,0:T(4,128)} %vel_hbm.1, f32[256,2,8,128]{3,2,1,0:T(8,128)} %bitcast.4, bf16[2,2,2,256,512]{4,3,2,1,0:T(8,128)(2,1)} %constant.2.clone.table_hbm, f32[128,128]{1,0:T(8,128)} %der_hbm.1, f32[128,128]{1,0:T(8,128)} %stiff_hbm.1, f32[4,128,128]{2,1,0:T(8,128)} %coup_hbm.1, ...), custom_call_target="tpu_custom_call" | custom-call | tf_op jit(solution)/shard_map/advect_helmholtz/pallas_call | solution.py:529
  29.4 1.3 %copy.11 = f32[512,8,128]{2,1,0:T(8,128)} copy(f32[512,8,128]{2,1,0:T(8,128)S(1)} %bitcast.3) | data formatting | bytes 4194304

commit v3 on v2

--- a/solution.py
+++ b/solution.py
@@ -18,6 +18,7 @@
 EARLY_CUTS = (0, 4, 8)
 REST_AT = 0
 LATE_CUTS = (0, 4, 6, 7, 8)
+PIECES = 9
 vmem_bytes = 67043328
 vmem_spare = 262144
 MESH = pl.DeviceIdType.MESH
@@ -48,9 +49,9 @@
     modes, groups, planes, elems, group_elems, rows, nodes,
     vel_hbm, prev_hbm, table_hbm, der_hbm, stiff_hbm, coup_hbm, reac_hbm, axial_hbm, near_hbm,
     outv,
-    vel, prev, table, der, stiff, coup, w_slope, w_apply, folded, sent, rhs, first, inverse,
-    halo_prev, halo_first, pairs, reac, axial, near,
-    lead_sem, vel_sem, table_sem, prev_sem, small_sem, y_send, y_recv, p_send, p_recv, f_send, f_recv,
+    vel, prev, table, der, taps, w_slope, w_apply, folded, sent, rhs, first, inverse,
+    halo_prev, halo_first, pairs, weights, near,
+    lead_sem, vel_sem, table_sem, small_sem, y_send, y_recv, p_send, p_recv, f_send, f_recv,
 ):
     half = planes // 2
     rim = group_elems // 4
@@ -64,6 +65,7 @@
         ]
         if start < stop
     ]
+    first_piece = [sum(len(cuts) - 1 for _, _, cuts in spans[:k]) for k in range(len(spans) + 1)]
     faces = faces_of(group_elems)
     me = lax.axis_index("mode")
     group = lax.axis_index("elem")
@@ -84,36 +86,43 @@
         return mode, (place - turn) % elems
 
     der_load = pltpu.make_async_copy(der_hbm, der, small_sem.at[0])
-    stiff_load = pltpu.make_async_copy(stiff_hbm, stiff, small_sem.at[1])
-    coup_load = pltpu.make_async_copy(coup_hbm, coup, small_sem.at[2])
+    stiff_load = pltpu.make_async_copy(stiff_hbm, taps.at[0], small_sem.at[1])
+    coup_load = pltpu.make_async_copy(coup_hbm, taps.at[pl.ds(1, 4)], small_sem.at[1])
 
     scalar_loads = [
-        pltpu.make_async_copy(src, dst, small_sem.at[3 + i])
-        for i, (src, dst) in enumerate([(reac_hbm, reac), (axial_hbm, axial), (near_hbm, near)])
+        pltpu.make_async_copy(src, dst, small_sem.at[i])
+        for i, src, dst in [
+            (2, reac_hbm, weights.at[0]), (2, axial_hbm, weights.at[1]), (3, near_hbm, near)
+        ]
     ]
 
     block = min(256, half)
 
     def vel_load(slot):
         return pltpu.make_async_copy(
-            vel_hbm.at[:, lax.rem(slot + skip(me), elems)], vel.at[slot], vel_sem.at[slot]
+            vel_hbm.at[:, lax.rem(slot + skip(me), elems)], vel.at[slot], vel_sem.at[min(slot, early)]
         )
 
     def lead_load(b, side):
         where = pl.ds(side * half + b * block, block)
         return pltpu.make_async_copy(
-            vel_hbm.at[where, skip(me)], vel.at[0, where], lead_sem.at[b, side]
-        )
+            vel_hbm.at[where, skip(me)], vel.at[0, where], lead_sem.at[b]
+        )
+
+    def wait_whole(ref, sem):
+        pltpu.make_async_copy(ref, ref, sem).wait()
 
     def table_load(step, parity):
         owner = lax.rem(me + step, modes)
         return pltpu.make_async_copy(
-            table_hbm.at[owner, parity], table.at[step, parity], table_sem.at[step, parity]
-        )
+            table_hbm.at[owner, parity], table.at[step, parity], table_sem.at[2 * step - 1 + parity]
+        )
+
+    own_table_load = pltpu.make_async_copy(table_hbm.at[me], table.at[0], table_sem.at[0])
 
     def prev_load(parity, e):
         return pltpu.make_async_copy(
-            prev_hbm.at[:, parity, e], prev.at[parity, e], prev_sem.at[parity, e]
+            prev_hbm.at[:, parity, e], prev.at[parity, e], small_sem.at[4]
         )
 
     steps = [*range(1, modes), 0]
@@ -130,8 +139,7 @@
     def start_rest():
         for slot in range(early, elems):
             vel_load(slot).start()
-        for parity in range(2):
-            table_load(0, parity).start()
+        own_table_load.start()
         for parity in range(2):
             for e in range(group_elems):
                 prev_load(parity, e).start()
@@ -158,11 +166,11 @@
 
     def halo_copies(source, halo, send, recv, c):
         right = pltpu.make_async_remote_copy(
-            source(c, 0), halo.at[0, c], send.at[0, c], recv.at[0, c],
+            source(c, 0), halo.at[0, c], send.at[0], recv.at[0, c],
             device_id={"elem": group + 1}, device_id_type=MESH,
         )
         left = pltpu.make_async_remote_copy(
-            source(c, 1), halo.at[1, c], send.at[1, c], recv.at[1, c],
+            source(c, 1), halo.at[1, c], send.at[1], recv.at[1, c],
             device_id={"elem": group - 1}, device_id_type=MESH,
         )
         return right, left
@@ -170,9 +178,13 @@
     def prev_rim(parity, side, i):
         return pltpu.make_async_remote_copy(
             prev_hbm.at[:, parity, (group_elems - rim) * (1 - side) + i],
-            halo_prev.at[side, parity, i], p_send.at[side, parity, i], p_recv.at[side, parity, i],
+            halo_prev.at[side, parity, i], p_send.at[side], p_recv.at[side, parity],
             device_id={"elem": group + 1 - 2 * side}, device_id_type=MESH,
         )
+
+    def wait_prev_rims(parity):
+        pl.when(has_left)(lambda: wait_whole(halo_prev.at[0, parity], p_recv.at[0, parity]))
+        pl.when(has_right)(lambda: wait_whole(halo_prev.at[1, parity], p_recv.at[1, parity]))
 
     def first_copies(c):
         def source(c, side):
@@ -184,11 +196,6 @@
         right, left = copies
         pl.when(has_left)(right.wait_recv)
         pl.when(has_right)(left.wait_recv)
-
-    def wait_halo_send(copies):
-        right, left = copies
-        pl.when(has_right)(right.wait_send)
-        pl.when(has_left)(left.wait_send)
 
     def each_prev_rim(parity, act_right, act_left):
         for i in range(rim):
@@ -214,12 +221,13 @@
     set_weights(w_slope, 0, der[...])
 
     def advect(slot):
-        if slot > 0:
+        if 0 < slot < early:
             vel_load(slot).wait()
+        if slot == early:
+            wait_whole(vel.at[pl.ds(early, elems - early)], vel_sem.at[early])
         for b in range(half // block):
             if slot == 0:
-                lead_load(b, 0).wait()
-                lead_load(b, 1).wait()
+                wait_whole(vel.at[0, pl.ds(0, 2 * block)], lead_sem.at[b])
             lower = vel[slot, pl.ds(b * block, block), :]
             upper = vel[slot, pl.ds(half + b * block, block), :]
             values = jnp.concatenate([lower, upper], axis=0)
@@ -259,7 +267,7 @@
         where = (pl.ds(cuts[n], cuts[n + 1] - cuts[n]), pl.ds(start, stop - start))
         return pltpu.make_async_remote_copy(
             sent.at[(step - 1,) + where], rhs.at[(me,) + where],
-            y_send.at[k, step - 1, n], y_recv.at[k, step - 1, n],
+            y_send.at[step - 1], y_recv.at[step - 1, first_piece[k] + n],
             device_id={"mode": lax.rem(me + step, modes)}, device_id_type=MESH,
         )
 
@@ -312,26 +320,23 @@
                     start_rest()
 
     each_prev_rim(1, (far_right, "start"), (far_left, "start"))
+    own_table_load.wait()
     for parity in range(2):
-        table_load(0, parity).wait()
         put_rows(rhs.at[me], parity, transform(0, parity, 0, elems), 0, elems)
 
-    stiff_load.wait()
-    coup_load.wait()
-    for load in scalar_loads:
-        load.wait()
-    set_weights(w_apply, 0, stiff[...])
+    wait_whole(taps, small_sem.at[1])
+    wait_whole(weights, small_sem.at[2])
+    scalar_loads[2].wait()
+    set_weights(w_apply, 0, taps[0])
     for f in range(faces):
-        matrix = coup[f] + coup[f + 1] if f == faces - 1 and faces < 4 else coup[f]
+        matrix = taps[f + 1] + taps[f + 2] if f == faces - 1 and faces < 4 else taps[f + 1]
         set_weights(w_apply, 2 * nodes * (f + 1), matrix)
     eye = lax.broadcasted_iota(jnp.int32, (nodes, nodes), 0) == lax.broadcasted_iota(
         jnp.int32, (nodes, nodes), 1
     )
-    diagonal = jnp.sum(jnp.where(eye, stiff[...], 0.0), axis=0, keepdims=True)
+    diagonal = jnp.sum(jnp.where(eye, taps[0], 0.0), axis=0, keepdims=True)
     pairs[zero_slot] = jnp.zeros((count, 2 * nodes), bf16)
-    for parity in range(2):
-        for e in range(group_elems):
-            prev_load(parity, e).wait()
+    wait_whole(prev, small_sem.at[4])
 
     def put_pair(slot, value):
         high, low = split(value)
@@ -386,13 +391,13 @@
             put_pair(rim + e, prev_rows(c, e))
         for parity in range(2):
             pl.when(c == parity * per_parity)(
-                lambda: each_prev_rim(parity, (has_left, "wait_recv"), (has_right, "wait_recv"))
+                lambda: wait_prev_rims(parity)
             )
         put_halo(prev_halo_rows, c)
         applied = apply()
         shift = shifts(c)
         for e in range(group_elems):
-            scaling = reac[e] + shift * axial[e]
+            scaling = weights[0, e] + shift * weights[1, e]
             recip = 1.0 / (diagonal + scaling)
             inverse[c, e] = recip
             value = prev_rows(c, e)
@@ -452,7 +457,7 @@
         shift = shifts(c)
         for e in range(group_elems):
             mode, slot = slot_of(e)
-            scaling = reac[e] + shift * axial[e]
+            scaling = weights[0, e] + shift * weights[1, e]
             value = first[c, e]
             part = applied[e * count : (e + 1) * count]
             start = (2 * (c % per_parity) * count + c // per_parity) * group_elems + e
@@ -464,17 +469,11 @@
     lax.fori_loop(0, 2, first_half, 0)
     lax.fori_loop(0, CHUNKS, second_sweep, 0)
 
-    def finish(c, carry):
-        wait_halo_send(first_copies(c))
-        return carry
-
-    lax.fori_loop(0, CHUNKS, finish, 0)
-    for parity in range(2):
-        each_prev_rim(parity, (has_right, "wait_send"), (has_left, "wait_send"))
-    for k in range(len(spans)):
-        for n in range(len(spans[k][2]) - 1):
-            for step in range(1, modes):
-                y_copy(step, k, n).wait_send()
+    for side, has in enumerate((has_right, has_left)):
+        pl.when(has)(lambda: wait_whole(halo_prev.at[side], p_send.at[side]))
+        pl.when(has)(lambda: wait_whole(halo_first.at[side], f_send.at[side]))
+    for step in range(1, modes):
+        wait_whole(sent.at[step - 1], y_send.at[step - 1])
 
 
 def faces_of(group_elems):
@@ -497,8 +496,7 @@
         pltpu.VMEM((2, group_elems, rows // 2, nodes), f32),
         pltpu.VMEM(tables.shape, bf16),
         pltpu.VMEM((nodes, nodes), f32),
-        pltpu.VMEM((nodes, nodes), f32),
-        pltpu.VMEM((4, nodes, nodes), f32),
+        pltpu.VMEM((5, nodes, nodes), f32),
         pltpu.VMEM((2 * nodes, 2 * nodes), bf16),
         pltpu.VMEM((taps * 2 * nodes, 2 * nodes), bf16),
         pltpu.VMEM((2, 2, half, elems * nodes), bf16),
@@ -509,21 +507,19 @@
         pltpu.VMEM((2, 2, rim, rows // 2, nodes), f32),
         pltpu.VMEM((2, CHUNKS, rim, count, nodes), f32),
         pltpu.VMEM((group_elems + 2 * rim + 1, count, 2 * nodes), bf16),
-        pltpu.SMEM((group_elems,), f32),
-        pltpu.SMEM((group_elems,), f32),
+        pltpu.SMEM((2, group_elems), f32),
         pltpu.SMEM((4, group_elems), jnp.int32),
     ]
     semaphores = [
-        dma((half // min(256, half), 2)),
-        dma((elems,)),
-        dma((modes, 2)),
-        dma((2, group_elems)),
-        dma((6,)),
-        dma((3, modes - 1, CHUNKS)),
-        dma((3, modes - 1, CHUNKS)),
-        dma((2, 2, rim)),
-        dma((2, 2, rim)),
-        dma((2, CHUNKS)),
+        dma((half // min(256, half),)),
+        dma((min(rim, elems) + 1,)),
+        dma((2 * modes - 1,)),
+        dma((5,)),
+        dma((modes - 1,)),
+        dma((modes - 1, PIECES)),
+        dma((2,)),
+        dma((2, 2)),
+        dma((2,)),
         dma((2, CHUNKS)),
     ]
     out = pl.pallas_call(

time: 31.1 us -> 30.3 us (0.974)
  Pallas kernels: 29.4 us -> 28.6 us
    pallas_call x1, Pallas kernels: 29.4 us -> 28.6 us  [body(): pl.pallas_call(run, out_shape=pltpu.VMEM((rows * group_elems, nodes), f32...]
where the time goes in v3:
time: 30.3 us; the launch traced here: 29.9 us
  Pallas kernels  28.6 us (94%)
  local copies, waits for them, and re-layouts  1.32 us (4%)
    pallas_call x1, Pallas kernels, body(): pl.pallas_call(run, out_shape=pltpu.VMEM((rows * group_elems, nodes), f32...  28.6 us
    unnamed x1, local copies, waits for them, and re-layouts  1.32 us

profile of v3, /device:TPU:0, one launch (start us, length us, event | category | flops | bytes accessed | tf_op | source)
XLA Modules:
  0.0 29.9 jit_solution(5251815958746552521)
XLA Ops:
  0.0 28.6 %advect_helmholtz.1 = f32[4096,128]{1,0:T(8,128)S(1)} custom-call(f32[1024,4,128]{2,1,0:T(4,128)} %vel_hbm.1, f32[256,2,8,128]{3,2,1,0:T(8,128)} %bitcast.4, bf16[2,2,2,256,512]{4,3,2,1,0:T(8,128)(2,1)} %constant.2.clone.table_hbm, f32[128,128]{1,0:T(8,128)} %der_hbm.1, f32[128,128]{1,0:T(8,128)} %stiff_hbm.1, f32[4,128,128]{2,1,0:T(8,128)} %coup_hbm.1, ...), custom_call_target="tpu_custom_call" | custom-call | tf_op jit(solution)/shard_map/advect_helmholtz/pallas_call | solution.py:525
  28.6 1.3 %copy.11 = f32[512,8,128]{2,1,0:T(8,128)} copy(f32[512,8,128]{2,1,0:T(8,128)S(1)} %bitcast.3) | data formatting | bytes 4194304

commit v4 on v3

--- a/solution.py
+++ b/solution.py
@@ -17,8 +17,8 @@
 LEAD_CUTS = (0, 1, 4, 8)
 EARLY_CUTS = (0, 4, 8)
 REST_AT = 0
-LATE_CUTS = (0, 4, 6, 7, 8)
-PIECES = 9
+LATE_CUTS = (0, 2, 4, 6, 7, 8)
+PIECES = 10
 vmem_bytes = 67043328
 vmem_spare = 262144
 MESH = pl.DeviceIdType.MESH
@@ -132,10 +132,6 @@
             lead_load(b, side).start()
     for step in range(1, modes):
         table_load(step, 0).start()
-    for slot in range(1, early):
-        vel_load(slot).start()
-    for step in range(1, modes):
-        table_load(step, 1).start()
     def start_rest():
         for slot in range(early, elems):
             vel_load(slot).start()
@@ -208,7 +204,7 @@
     near_right = jnp.logical_and(has_right, lax.rem(group, 4) != 3)
     near_left = jnp.logical_and(has_left, lax.rem(group, 4) != 0)
     left_local = me == 0
-    right_local = me == modes - 1
+    right_local = jnp.logical_and(me == modes - 1, lax.rem(group, 4) != 3)
     held_back = lax.rem(group, 2) == 1
 
     def set_weights(ref, at, matrix):
@@ -218,6 +214,10 @@
             ref[pl.ds(at + part * nodes, nodes), pl.ds(nodes, nodes)] = low
 
     der_load.wait()
+    for slot in range(1, early):
+        vel_load(slot).start()
+    for step in range(1, modes):
+        table_load(step, 1).start()
     set_weights(w_slope, 0, der[...])
 
     def advect(slot):

time: 30.3 us -> 29.9 us (0.987)
  Pallas kernels: 28.6 us -> 28.2 us
    pallas_call x1, Pallas kernels: 28.6 us -> 28.2 us  [body(): pl.pallas_call(run, out_shape=pltpu.VMEM((rows * group_elems, nodes), f32...]
where the time goes in v4:
time: 29.9 us; the launch traced here: 29.5 us
  Pallas kernels  28.2 us (94%)
  local copies, waits for them, and re-layouts  1.32 us (4%)
    pallas_call x1, Pallas kernels, body(): pl.pallas_call(run, out_shape=pltpu.VMEM((rows * group_elems, nodes), f32...  28.2 us
    unnamed x1, local copies, waits for them, and re-layouts  1.32 us

profile of v4, /device:TPU:0, one launch (start us, length us, event | category | flops | bytes accessed | tf_op | source)
XLA Modules:
  0.0 29.5 jit_solution(12376571800547303932)
XLA Ops:
  0.0 28.2 %advect_helmholtz.1 = f32[4096,128]{1,0:T(8,128)S(1)} custom-call(f32[1024,4,128]{2,1,0:T(4,128)} %vel_hbm.1, f32[256,2,8,128]{3,2,1,0:T(8,128)} %bitcast.4, bf16[2,2,2,256,512]{4,3,2,1,0:T(8,128)(2,1)} %constant.2.clone.table_hbm, f32[128,128]{1,0:T(8,128)} %der_hbm.1, f32[128,128]{1,0:T(8,128)} %stiff_hbm.1, f32[4,128,128]{2,1,0:T(8,128)} %coup_hbm.1, ...), custom_call_target="tpu_custom_call" | custom-call | tf_op jit(solution)/shard_map/advect_helmholtz/pallas_call | solution.py:525
  28.2 1.3 %copy.11 = f32[512,8,128]{2,1,0:T(8,128)} copy(f32[512,8,128]{2,1,0:T(8,128)S(1)} %bitcast.3) | data formatting | bytes 4194304

commit v5 on v4

--- a/solution.py
+++ b/solution.py
@@ -18,7 +18,7 @@
 EARLY_CUTS = (0, 4, 8)
 REST_AT = 0
 LATE_CUTS = (0, 2, 4, 6, 7, 8)
-PIECES = 10
+PIECES = 7
 vmem_bytes = 67043328
 vmem_spare = 262144
 MESH = pl.DeviceIdType.MESH
@@ -65,7 +65,6 @@
         ]
         if start < stop
     ]
-    first_piece = [sum(len(cuts) - 1 for _, _, cuts in spans[:k]) for k in range(len(spans) + 1)]
     faces = faces_of(group_elems)
     me = lax.axis_index("mode")
     group = lax.axis_index("elem")
@@ -160,13 +159,16 @@
     def _():
         pl.semaphore_signal(barrier, inc=1, device_id={"elem": group + 1}, device_id_type=MESH)
 
+    def halo_slot(c):
+        return jnp.maximum(c - per_parity + 1, 0)
+
     def halo_copies(source, halo, send, recv, c):
         right = pltpu.make_async_remote_copy(
-            source(c, 0), halo.at[0, c], send.at[0], recv.at[0, c],
+            source(c, 0), halo.at[0, c], send.at[0], recv.at[0, halo_slot(c)],
             device_id={"elem": group + 1}, device_id_type=MESH,
         )
         left = pltpu.make_async_remote_copy(
-            source(c, 1), halo.at[1, c], send.at[1], recv.at[1, c],
+            source(c, 1), halo.at[1, c], send.at[1], recv.at[1, halo_slot(c)],
             device_id={"elem": group - 1}, device_id_type=MESH,
         )
         return right, left
@@ -262,12 +264,16 @@
                     j * count : (j + 1) * count, at : at + nodes
                 ]
 
+    def piece_slot(k, n):
+        start, _, cuts = spans[k]
+        return 2 + n if start >= early else int(cuts[n] >= per_parity)
+
     def y_copy(step, k, n):
         start, stop, cuts = spans[k]
         where = (pl.ds(cuts[n], cuts[n + 1] - cuts[n]), pl.ds(start, stop - start))
         return pltpu.make_async_remote_copy(
             sent.at[(step - 1,) + where], rhs.at[(me,) + where],
-            y_send.at[step - 1], y_recv.at[step - 1, first_piece[k] + n],
+            y_send.at[step - 1], y_recv.at[step - 1, piece_slot(k, n)],
             device_id={"mode": lax.rem(me + step, modes)}, device_id_type=MESH,
         )
 
@@ -278,6 +284,18 @@
                     y_copy(step, k, n).start()
 
     def wait_pieces(late, c, begin=0, end=CHUNKS, also=True):
+        for parity in range(2):
+            at = parity * per_parity
+            if not late and begin <= at < end:
+                @pl.when(jnp.logical_and(c == at, also))
+                def _():
+                    for step in range(1, modes):
+                        mode = lax.rem(me + modes - step, modes)
+                        whole = rhs.at[mode, pl.ds(at, per_parity), pl.ds(0, early)]
+                        wait_whole(whole, y_recv.at[step - 1, parity])
+
+        if not late:
+            return
         for at in range(begin, end):
             due = [
                 (k, n)
@@ -443,7 +461,13 @@
         for slot in range(early, elems):
             e = element_of(me, slot)
             put_pair(rim + e, first[c, e])
-        wait_halo_recv(first_copies(c))
+        @pl.when(c == 0)
+        def _():
+            for side, has in enumerate((has_left, has_right)):
+                half_rows = halo_first.at[side, pl.ds(0, per_parity)]
+                pl.when(has)(lambda: wait_whole(half_rows, f_recv.at[side, 0]))
+
+        pl.when(c >= per_parity)(lambda: wait_halo_recv(first_copies(c)))
         put_halo(lambda side, c, i: halo_first[side, c, i], c)
         if early < elems:
             wait_pieces(True, c)
@@ -520,7 +544,7 @@
         dma((2,)),
         dma((2, 2)),
         dma((2,)),
-        dma((2, CHUNKS)),
+        dma((2, CHUNKS // 2 + 1)),
     ]
     out = pl.pallas_call(
         run,

time: 29.9 us -> 30.3 us (1.013)
  the two profiles are of different devices: /device:TPU:0 before, /device:TPU:9 now
where the time goes in v5:
time: 30.3 us; the launch traced here: 30.1 us
  Pallas kernels  28.8 us (95%)
  local copies, waits for them, and re-layouts  1.32 us (4%)
    pallas_call x1, Pallas kernels, body(): pl.pallas_call(run, out_shape=pltpu.VMEM((rows * group_elems, nodes), f32...  28.8 us
    unnamed x1, local copies, waits for them, and re-layouts  1.32 us

profile of v5, /device:TPU:9, one launch (start us, length us, event | category | flops | bytes accessed | tf_op | source)
XLA Modules:
  0.0 30.1 jit_solution(18343193333248466094)
XLA Ops:
  0.0 28.8 %advect_helmholtz.1 = f32[4096,128]{1,0:T(8,128)S(1)} custom-call(f32[1024,4,128]{2,1,0:T(4,128)} %vel_hbm.1, f32[256,2,8,128]{3,2,1,0:T(8,128)} %bitcast.4, bf16[2,2,2,256,512]{4,3,2,1,0:T(8,128)(2,1)} %constant.2.clone.table_hbm, f32[128,128]{1,0:T(8,128)} %der_hbm.1, f32[128,128]{1,0:T(8,128)} %stiff_hbm.1, f32[4,128,128]{2,1,0:T(8,128)} %coup_hbm.1, ...), custom_call_target="tpu_custom_call" | custom-call | tf_op jit(solution)/shard_map/advect_helmholtz/pallas_call | solution.py:549
  28.8 1.3 %copy.11 = f32[512,8,128]{2,1,0:T(8,128)} copy(f32[512,8,128]{2,1,0:T(8,128)S(1)} %bitcast.3) | data formatting | bytes 4194304
